TPU v7x, 256 devices: a whole 4x4x8 slice. The times are simulated.
256 devices in a mesh: env: 16 (over x, y_lo, core), pts: 16 (over y_hi, z).
Axes of the slice: x: 4, y: 4 (y_hi: 2, y_lo: 2; y = y_hi * 2 + y_lo), z: 8, core: 2. Of those that a mesh axis runs over, the one named last changes fastest.
Arguments:
- descriptors: float32 [1024, 16384], P('pts', 'env'), may hold values from -6 to 6
- env_weight: float32 [16384], P('env'), may hold values from 0.25 to 4
- points: float32 [2560, 1024], P('pts', 'env'), may hold values from -6 to 6
Outputs:
- panel_factor: float32 [2560, 512], P('env', 'pts')
- trailing: float32 [2048, 2048], P('env', 'pts')
All inputs are finite; a program needn't handle non-finite values.
Results may differ from a plain program's by a relative error of at most 0.0003.
Values sent between devices are 32-bit elements; how exact they have to be, the bound alone decides.
A program may use at most 64 MiB of HBM per device.

v0:
```python
import jax
import jax.numpy as jnp
from jax import lax
from jax.sharding import Mesh
from jax.sharding import PartitionSpec as P

PANEL = 512
PTS = ("pts_0", "pts_1")
ENV_PTS = ("env", "pts_0", "pts_1")


def joined_along(blocks, dim):
    lengths = list(blocks.shape[1:])
    lengths[dim] *= blocks.shape[0]
    return jnp.moveaxis(blocks, 0, dim).reshape(lengths)


def gather_in_order(shard, axes, order):
    blocks = shard[None]
    for k in order:
        blocks = lax.all_gather(blocks, axes[k], axis=0, tiled=True)
    held = [lax.axis_size(axes[k]) for k in reversed(order)]
    blocks = blocks.reshape(*held, *shard.shape)
    turned = sorted(range(len(order)), key=lambda place: order[len(order) - 1 - place])
    return blocks.transpose(*turned, *range(len(order), blocks.ndim)).reshape(-1, *shard.shape)


def gathered_by_axis(shard, axes, order, dim):
    return joined_along(gather_in_order(shard, axes, order), dim)


def cut_along(shard, dim, count):
    before, after = (shard.shape[:dim], shard.shape[dim + 1 :])
    return jnp.moveaxis(shard.reshape(*before, count, -1, *after), dim, 0)


def summed_on_arrival(shard, axis, dim):
    count = lax.axis_size(axis)
    blocks = lax.all_to_all(cut_along(shard, dim, count), axis, 0, 0, tiled=True)
    return jnp.sum(blocks, axis=0)


def cubed_kernel(features, targets):
    dots = lax.dot_general(
        features,
        targets,
        (((0,), (1,)), ((), ())),
        precision=lax.Precision.HIGH,
        preferred_element_type=jnp.float32,
    )
    scaled = dots / jnp.sqrt(jnp.float32(features.shape[0]))
    return 0.25 * scaled * scaled * scaled


def local_points(count, device, devices, block_size):
    positions = jnp.arange(count, dtype=jnp.int32)
    return block_size * (devices * (positions // block_size) + device) + positions % block_size


def local(descriptors, env_weight, points):
    env_count = lax.axis_size("env")
    pts_count = lax.axis_size(PTS)
    env_rank = lax.axis_index("env")
    pts_rank = lax.axis_index(PTS)
    features = gathered_by_axis(descriptors, PTS, (0, 1), 0)
    own_points = lax.all_gather(points, "env", axis=1, tiled=True)
    cols_dev = own_points.shape[0]
    total_points = cols_dev * pts_count
    rows_dev = total_points // env_count
    row_block = PANEL // env_count
    col_block = PANEL // pts_count
    cycles = total_points // PANEL
    own_tile = cubed_kernel(features, own_points)
    weighted = own_tile * env_weight[:, None]
    partial_gram = lax.dot_general(
        lax.all_gather(own_tile, PTS, axis=1, tiled=True),
        weighted,
        (((0,), (0,)), ((), ())),
        precision=lax.Precision.HIGH,
        preferred_element_type=jnp.float32,
    )
    partial_gram = partial_gram / jnp.float32(descriptors.shape[1] * env_count)
    natural = (
        partial_gram.reshape(pts_count, cycles, col_block, cols_dev)
        .transpose(1, 0, 2, 3)
        .reshape(total_points, cols_dev)
    )
    by_rows = (
        natural.reshape(cycles, env_count, row_block, cols_dev)
        .transpose(1, 0, 2, 3)
        .reshape(total_points, cols_dev)
    )
    gram_block = summed_on_arrival(by_rows, "env", 0)
    row_ids = local_points(rows_dev, env_rank, env_count, row_block)
    col_ids = local_points(cols_dev, pts_rank, pts_count, col_block)
    gram_block = gram_block + (row_ids[:, None] == col_ids[None, :]).astype(jnp.float32)
    panel_rows = lax.all_gather(gram_block[:, :col_block], PTS, axis=1, tiled=True)
    leading = lax.all_gather(panel_rows[:row_block], "env", axis=0, tiled=True)
    low_factor = jnp.linalg.cholesky(leading)
    row_factor = jax.scipy.linalg.solve_triangular(low_factor, panel_rows.T, lower=True).T
    panel_out = lax.dynamic_slice_in_dim(row_factor, pts_rank * col_block, col_block, 1)
    top_rows = lax.all_gather(gram_block[:row_block, :], "env", axis=0, tiled=True)
    side_factor = jax.scipy.linalg.solve_triangular(low_factor, top_rows, lower=True).T[col_block:]
    update = lax.dot_general(
        row_factor[row_block:],
        side_factor,
        (((1,), (1,)), ((), ())),
        precision=lax.Precision.HIGHEST,
        preferred_element_type=jnp.float32,
    )
    trailing = gram_block[row_block:, col_block:] - update
    return (panel_out, trailing)


def solution(mesh):
    finer = Mesh(mesh.devices.reshape(mesh.shape["env"], 2, 8), ("env", "pts_0", "pts_1"))
    placed = (P(PTS, "env"), P("env"), P(PTS, "env"))
    return jax.shard_map(
        local,
        mesh=finer,
        in_specs=placed,
        out_specs=(P("env", PTS), P("env", PTS)),
        check_vma=False,
    )
```

profile of v0, /device:TPU:1, one launch (start us, length us, event | category | flops | bytes accessed | tf_op | source)
XLA Modules:
  0.0 520.1 jit_solution(16651984961840194268)
XLA Ops:
  7.2 12.0 %all-gather = f32[128,1024]{1,0:T(8,128)} all-gather(f32[64,1024]{1,0:T(8,128)} %param.5), channel_id=2, replica_groups=mesh['env'=16,'pts_0'=2,'pts_1'=8] {'pts_0'}, dimensions={0}, use_global_device_ids=true | all-gather | bytes 786432 | tf_op jit(solution)/shard_map/all_gather | solution.py:21
  19.3 23.6 %all_gather.23 = f32[160,1024]{0,1:T(8,128)S(1)} all-gather(f32[160,64]{0,1:T(8,128)} %param.7), channel_id=1, replica_groups=mesh['env'=16,'pts_0'=2,'pts_1'=8] {'env'}, dimensions={1}, use_global_device_ids=true | all-gather | bytes 696320 | tf_op jit(solution)/shard_map/all_gather | solution.py:66
  42.9 33.4 %all-gather.5.cloned.1.call-done = f32[16,64,1024]{2,1,0:T(8,128)} async-done(((f32[2,64,1024]{2,1,0:T(8,128)}), f32[16,64,1024]{2,1,0:T(8,128)}) %all-gather.5.cloned.1.call-update) | async-done | bytes 4194320 | tf_op jit(solution)/shard_map/all_gather | solution.py:21
  76.3 2.5 copy.28
  78.8 2.3 multiply_multiply_fusion
  81.1 154.6 %all-gather.7.cloned.1.call-done = f32[1024,2560]{0,1:T(8,128)} async-done(((f32[1024,160]{0,1:T(8,128)}), f32[1024,2560]{0,1:T(8,128)}) %all-gather.7.cloned.1.call-update) | async-done | bytes 10485776 | tf_op jit(solution)/shard_map/all_gather | solution.py:76
  235.7 10.6 %convolution_multiply_fusion = f32[2560,160]{0,1:T(8,128)} fusion(f32[1024,2560]{0,1:T(8,128)} %all-gather.7.cloned.1.call-done, f32[1024]{0:T(1024)S(1)} %copy-done.2, f32[1024,160]{0,1:T(8,128)S(1)} %get-tuple-element.55), kind=kOutput, calls=%fused_computation.2 | convolution fusion | flops 2517811200 | bytes 12783616 | tf_op jit(solution)/shard_map/dot_general | solution.py:75
  246.3 2.6 reshape_reshape_reshape.3
  248.9 3.0 copy.29
  251.9 5.7 %all-to-all-start = ((f32[16,160,160]{1,2,0:T(8,128)}), f32[16,160,160]{1,2,0:T(8,128)S(1)}, u32[]{:S(2)}, u32[]{:S(2)}) async-start(f32[16,160,160]{1,2,0:T(8,128)} %copy.29), calls=%async_computation | async-start | bytes 5242880 | tf_op jit(solution)/shard_map/all_to_all | solution.py:39
  257.6 33.3 %all-to-all-done = f32[16,160,160]{1,2,0:T(8,128)S(1)} async-done(((f32[16,160,160]{1,2,0:T(8,128)}), f32[16,160,160]{1,2,0:T(8,128)S(1)}, u32[]{:S(2)}, u32[]{:S(2)}) %all-to-all-start) | async-done | bytes 1638432 | tf_op jit(solution)/shard_map/all_to_all | solution.py:39
  291.4 34.4 %all_gather.25 = f32[160,512]{0,1:T(8,128)S(1)} all-gather(f32[160,32]{0,1:T(8,128)S(1)} %copy.31), channel_id=1, replica_groups=mesh['env'=16,'pts_0'=2,'pts_1'=8] {'pts_0','pts_1'}, dimensions={1}, use_global_device_ids=true | all-gather | bytes 348160 | tf_op jit(solution)/shard_map/all_gather | solution.py:97
  327.3 28.4 %all_gather.27 = f32[512,160]{1,0:T(8,128)S(1)} all-gather(f32[32,160]{1,0:T(8,128)S(1)} %slice.144), channel_id=1, replica_groups=mesh['env'=16,'pts_0'=2,'pts_1'=8] {'env'}, dimensions={0}, use_global_device_ids=true | all-gather | bytes 348160 | tf_op jit(solution)/shard_map/all_gather | solution.py:102
  358.2 6.9 %all-gather.9.cloned.1.call-done = f32[512,512]{1,0:T(8,128)} async-done(((f32[32,512]{1,0:T(8,128)}), f32[512,512]{1,0:T(8,128)}) %all-gather.9.cloned.1.call-update) | async-done | bytes 1048592 | tf_op jit(solution)/shard_map/all_gather | solution.py:98
  368.2 11.7 %cholesky.104 = f32[128,128]{1,0:T(8,128)S(1)} custom-call(f32[128,128]{1,0:T(8,128)S(1)} %cholesky.266), custom_call_target="Cholesky" | custom-call | tf_op jit(solution)/shard_map/jit(cholesky)/cholesky | solution.py:99
  380.0 9.8 %custom-call.30 = f32[1,128,128]{1,2,0:T(8,128)S(1)} custom-call(f32[1,128,128]{2,1,0:T(8,128)S(1)} %get-tuple-element.53), custom_call_target="InvertDiagBlocksLowerTriangular" | custom-call | tf_op jit(solution)/shard_map/jit(cholesky)/cholesky | solution.py:99
  390.5 11.7 %cholesky.217 = f32[128,128]{1,0:T(8,128)S(1)} custom-call(f32[128,128]{1,0:T(8,128)S(1)} %cholesky.270), custom_call_target="Cholesky" | custom-call | tf_op jit(solution)/shard_map/jit(cholesky)/cholesky | solution.py:99
  402.3 10.0 %custom-call.31 = f32[1,128,128]{1,2,0:T(8,128)S(1)} custom-call(f32[1,128,128]{2,1,0:T(8,128)S(1)} %get-tuple-element.50), custom_call_target="InvertDiagBlocksLowerTriangular" | custom-call | tf_op jit(solution)/shard_map/jit(cholesky)/cholesky | solution.py:99
  412.9 11.7 %cholesky.238 = f32[128,128]{1,0:T(8,128)S(1)} custom-call(f32[128,128]{1,0:T(8,128)S(1)} %cholesky.275), custom_call_target="Cholesky" | custom-call | tf_op jit(solution)/shard_map/jit(cholesky)/cholesky | solution.py:99
  424.7 9.8 %custom-call.32 = f32[1,128,128]{1,2,0:T(8,128)S(1)} custom-call(f32[1,128,128]{2,1,0:T(8,128)S(1)} %get-tuple-element.47), custom_call_target="InvertDiagBlocksLowerTriangular" | custom-call | tf_op jit(solution)/shard_map/jit(cholesky)/cholesky | solution.py:99
  435.1 11.9 %cholesky.255 = f32[128,128]{1,0:T(8,128)S(1)} custom-call(f32[128,128]{1,0:T(8,128)S(1)} %convolution_subtract_fusion.9), custom_call_target="Cholesky" | custom-call | tf_op jit(solution)/shard_map/jit(cholesky)/cholesky | solution.py:99
  453.0 10.9 %while.4 = (s32[]{:T(128)}, f32[512,512]{1,0:T(8,128)S(1)}, s32[4,2]{0,1:T(2,128)S(1)}, f32[4,128,128]{2,1,0:T(8,128)}, s32[]{:T(128)}) while((s32[]{:T(128)}, f32[512,512]{1,0:T(8,128)S(1)}, s32[4,2]{0,1:T(2,128)S(1)}, f32[4,128,128]{2,1,0:T(8,128)}, s32[]{:T(128)}) %tuple.45), condition=%wide.while_cond, body=%wide.while_body.sunk | while | flops 2 | bytes 132205 | solution.py:100
  456.4 2.1 bitcast_dynamic-update-slice_fusion.2
  463.8 40.1 %custom-call.34 = f32[4,128,128]{1,2,0:T(8,128)S(1)} custom-call(f32[4,128,128]{2,1,0:T(8,128)} %get-tuple-element.17), custom_call_target="InvertDiagBlocksLowerTriangular" | custom-call | tf_op jit(solution)/shard_map/jit(_solve_triangular)/triangular_solve | solution.py:100
  (80 shorter events, 31.2 us)
Async XLA Ops:
  7.2 69.1 %all-gather.5.cloned.1.call-start = ((), (), s32[]{:S(2)}) async-start(), calls=%async_computation.1 | async-start | bytes 4718592 | tf_op jit(solution)/shard_map/all_gather | solution.py:21
  19.2 216.5 %all-gather.7.cloned.1.call-start = ((), (), s32[]{:S(2)}) async-start(), calls=%async_computation.2 | async-start | bytes 11141120 | tf_op jit(solution)/shard_map/all_gather | solution.py:76
  78.8 156.9 %copy-start.2 = (f32[1024]{0:T(1024)S(1)}, f32[1024]{0:T(1024)}, u32[]{:S(2)}) copy-start(f32[1024]{0:T(1024)} %param.6) | copy-start | bytes 12292
  251.9 39.1 %all-to-all-start = ((f32[16,160,160]{1,2,0:T(8,128)}), f32[16,160,160]{1,2,0:T(8,128)S(1)}, u32[]{:S(2)}, u32[]{:S(2)}) async-start(f32[16,160,160]{1,2,0:T(8,128)} %copy.29), calls=%async_computation | async-start | bytes 5242880 | tf_op jit(solution)/shard_map/all_to_all | solution.py:39
  257.6 107.6 %all-gather.9.cloned.1.call-start = ((), (), s32[]{:S(2)}) async-start(), calls=%async_computation.3 | async-start | bytes 1114112 | tf_op jit(solution)/shard_map/all_gather | solution.py:98
  291.3 66.9 %copy-start.1 = (f32[160,160]{1,0:T(8,128)}, f32[160,160]{1,0:T(8,128)S(1)}, u32[]{:S(2)}) copy-start(f32[160,160]{1,0:T(8,128)S(1)} %convert_add_fusion) | copy-start | bytes 307204
  355.8 0.8 copy-start
Sparse Core Ops, SparseCore 0:
  19.3 56.9 all-gather.4
  81.2 154.4 all-gather.6
  326.7 38.3 all-gather.8
where the time goes:
time: 528 us; the launch traced here: 520 us
  waiting for transfers between devices  228 us (43%)
  other arithmetic  122 us (23%)
  blocking collectives  98.4 us (19%)
  local copies, waits for them, and re-layouts  25.6 us (5%)
  matrix products  23.1 us (4%)
  between operations  16.8 us (3%)
  starting transfers between devices  5.81 us (1%)
    all_gather x1, waiting for transfers between devices, local(): lax.all_gather(own_tile, PTS, axis=1, tiled=True)  155 us
    another operation x15, other arithmetic, local(): low_factor = jnp.linalg.cholesky(leading)  79.4 us
    another operation x4, other arithmetic, local(): jax.scipy.linalg.solve_triangular(low_factor, panel_rows.T, lower=True)  40.8 us
    all_gather x1, blocking collectives, local(): lax.all_gather(gram_block[:, :col_block], PTS, axis=1, tiled=True)  34.4 us
    all_gather x1, waiting for transfers between devices, gather_in_order(): blocks = lax.all_gather(blocks, axes[k], axis=0, tiled=True)  33.4 us
    all_to_all x1, waiting for transfers between devices, summed_on_arrival(): lax.all_to_all(cut_along(shard, dim, count), axis, 0, 0, tiled=True)  33.3 us
    all_gather x1, blocking collectives, local(): lax.all_gather(gram_block[:row_block, :], 'env', axis=0, tiled=True)  28.4 us
    all_gather x1, blocking collectives, local(): own_points = lax.all_gather(points, 'env', axis=1, tiled=True)  23.6 us
  transfers between devices with their start and end apart: 4, of which 4 were waited for; matrix products, arithmetic and copies ran while one was open for 0% of the time, Pallas kernels for 0%

commit v1 on v0

--- a/solution.py
+++ b/solution.py
@@ -94,7 +94,10 @@
     row_ids = local_points(rows_dev, env_rank, env_count, row_block)
     col_ids = local_points(cols_dev, pts_rank, pts_count, col_block)
     gram_block = gram_block + (row_ids[:, None] == col_ids[None, :]).astype(jnp.float32)
-    panel_rows = lax.all_gather(gram_block[:, :col_block], PTS, axis=1, tiled=True)
+    panel_rows = jnp.concatenate(
+        lax.all_to_all(jnp.stack([gram_block[:, :col_block]] * lax.axis_size(PTS)), PTS, 0, 0),
+        axis=1,
+    )
     leading = lax.all_gather(panel_rows[:row_block], "env", axis=0, tiled=True)
     low_factor = jnp.linalg.cholesky(leading)
     row_factor = jax.scipy.linalg.solve_triangular(low_factor, panel_rows.T, lower=True).T

time: 528 us -> 511 us (0.968)
  blocking collectives: 98.4 us -> 80.5 us
    all_gather x1 -> x0, blocking collectives: 34.4 us -> none  [local(): lax.all_gather(gram_block[:, :col_block], PTS, axis=1, tiled=True)]
    all_to_all x0 -> x1, blocking collectives: none -> 21.4 us  [local(): lax.all_to_all(jnp.stack([gram_block[:, :col_block]] * lax.axis_size(PTS)...]
where the time goes in v1:
time: 511 us; the launch traced here: 503 us
  waiting for transfers between devices  229 us (45%)
  other arithmetic  122 us (24%)
  blocking collectives  80.5 us (16%)
  local copies, waits for them, and re-layouts  25.7 us (5%)
  matrix products  23.1 us (5%)
  between operations  16.8 us (3%)
  starting transfers between devices  5.81 us (1%)
    all_gather x1, waiting for transfers between devices, local(): lax.all_gather(own_tile, PTS, axis=1, tiled=True)  155 us
    another operation x15, other arithmetic, local(): low_factor = jnp.linalg.cholesky(leading)  79.4 us
    another operation x4, other arithmetic, local(): jax.scipy.linalg.solve_triangular(low_factor, panel_rows.T, lower=True)  40.8 us
    all_gather x1, waiting for transfers between devices, gather_in_order(): blocks = lax.all_gather(blocks, axes[k], axis=0, tiled=True)  33.4 us
    all_to_all x1, waiting for transfers between devices, summed_on_arrival(): lax.all_to_all(cut_along(shard, dim, count), axis, 0, 0, tiled=True)  33.3 us
    all_gather x1, blocking collectives, local(): own_points = lax.all_gather(points, 'env', axis=1, tiled=True)  23.6 us
    all_gather x1, blocking collectives, local(): lax.all_gather(gram_block[:row_block, :], 'env', axis=0, tiled=True)  23.5 us
    all_to_all x1, blocking collectives, local(): lax.all_to_all(jnp.stack([gram_block[:, :col_block]] * lax.axis_size(PTS)...  21.4 us
  transfers between devices with their start and end apart: 4, of which 4 were waited for; matrix products, arithmetic and copies ran while one was open for 0% of the time, Pallas kernels for 0%

profile of v1, /device:TPU:1, one launch (start us, length us, event | category | flops | bytes accessed | tf_op | source)
XLA Modules:
  0.0 503.1 jit_solution(5914022234829544233)
XLA Ops:
  7.2 12.0 %all-gather = f32[128,1024]{1,0:T(8,128)} all-gather(f32[64,1024]{1,0:T(8,128)} %param.5), channel_id=2, replica_groups=mesh['env'=16,'pts_0'=2,'pts_1'=8] {'pts_0'}, dimensions={0}, use_global_device_ids=true | all-gather | bytes 786432 | tf_op jit(solution)/shard_map/all_gather | solution.py:21
  19.3 23.6 %all_gather.20 = f32[160,1024]{0,1:T(8,128)S(1)} all-gather(f32[160,64]{0,1:T(8,128)} %param.7), channel_id=1, replica_groups=mesh['env'=16,'pts_0'=2,'pts_1'=8] {'env'}, dimensions={1}, use_global_device_ids=true | all-gather | bytes 696320 | tf_op jit(solution)/shard_map/all_gather | solution.py:66
  42.9 33.4 %all-gather.5.cloned.1.call-done = f32[16,64,1024]{2,1,0:T(8,128)} async-done(((f32[2,64,1024]{2,1,0:T(8,128)}), f32[16,64,1024]{2,1,0:T(8,128)}) %all-gather.5.cloned.1.call-update) | async-done | bytes 4194320 | tf_op jit(solution)/shard_map/all_gather | solution.py:21
  76.3 2.5 copy.33
  78.8 2.3 multiply_multiply_fusion
  81.1 154.6 %all-gather.7.cloned.1.call-done = f32[1024,2560]{0,1:T(8,128)} async-done(((f32[1024,160]{0,1:T(8,128)}), f32[1024,2560]{0,1:T(8,128)}) %all-gather.7.cloned.1.call-update) | async-done | bytes 10485776 | tf_op jit(solution)/shard_map/all_gather | solution.py:76
  235.7 10.6 %convolution_multiply_fusion = f32[2560,160]{0,1:T(8,128)} fusion(f32[1024,2560]{0,1:T(8,128)} %all-gather.7.cloned.1.call-done, f32[1024]{0:T(1024)S(1)} %copy-done.2, f32[1024,160]{0,1:T(8,128)S(1)} %get-tuple-element.57), kind=kOutput, calls=%fused_computation.2 | convolution fusion | flops 2517811200 | bytes 12783616 | tf_op jit(solution)/shard_map/dot_general | solution.py:75
  246.3 2.6 reshape_reshape_reshape.3
  248.9 3.0 copy.34
  251.9 5.7 %all-to-all-start = ((f32[16,160,160]{1,2,0:T(8,128)}), f32[16,160,160]{1,2,0:T(8,128)S(1)}, u32[]{:S(2)}, u32[]{:S(2)}) async-start(f32[16,160,160]{1,2,0:T(8,128)} %copy.34), calls=%async_computation | async-start | bytes 5242880 | tf_op jit(solution)/shard_map/all_to_all | solution.py:39
  257.6 33.3 %all-to-all-done = f32[16,160,160]{1,2,0:T(8,128)S(1)} async-done(((f32[16,160,160]{1,2,0:T(8,128)}), f32[16,160,160]{1,2,0:T(8,128)S(1)}, u32[]{:S(2)}, u32[]{:S(2)}) %all-to-all-start) | async-done | bytes 1638432 | tf_op jit(solution)/shard_map/all_to_all | solution.py:39
  291.5 21.4 %all_to_all.10 = f32[16,160,32]{1,2,0:T(8,128)S(1)} all-to-all(f32[16,160,32]{1,2,0:T(8,128)S(1)} %stack.2), channel_id=1, replica_groups=mesh['env'=16,'pts_0'=2,'pts_1'=8] {'pts_0','pts_1'}, dimensions={0} | all-to-all | bytes 655360 | tf_op jit(solution)/shard_map/all_to_all | solution.py:98
  314.3 23.5 %all_gather.23 = f32[512,160]{1,0:T(8,128)S(1)} all-gather(f32[32,160]{1,0:T(8,128)S(1)} %slice.148), channel_id=1, replica_groups=mesh['env'=16,'pts_0'=2,'pts_1'=8] {'env'}, dimensions={0}, use_global_device_ids=true | all-gather | bytes 348160 | tf_op jit(solution)/shard_map/all_gather | solution.py:105
  340.3 7.9 %all-gather.9.cloned.1.call-done = f32[512,512]{1,0:T(8,128)} async-done(((f32[32,512]{1,0:T(8,128)}), f32[512,512]{1,0:T(8,128)}) %all-gather.9.cloned.1.call-update) | async-done | bytes 1048592 | tf_op jit(solution)/shard_map/all_gather | solution.py:101
  351.2 11.7 %cholesky.104 = f32[128,128]{1,0:T(8,128)S(1)} custom-call(f32[128,128]{1,0:T(8,128)S(1)} %cholesky.266), custom_call_target="Cholesky" | custom-call | tf_op jit(solution)/shard_map/jit(cholesky)/cholesky | solution.py:102
  363.1 9.8 %custom-call.30 = f32[1,128,128]{1,2,0:T(8,128)S(1)} custom-call(f32[1,128,128]{2,1,0:T(8,128)S(1)} %get-tuple-element.55), custom_call_target="InvertDiagBlocksLowerTriangular" | custom-call | tf_op jit(solution)/shard_map/jit(cholesky)/cholesky | solution.py:102
  373.6 11.7 %cholesky.217 = f32[128,128]{1,0:T(8,128)S(1)} custom-call(f32[128,128]{1,0:T(8,128)S(1)} %cholesky.270), custom_call_target="Cholesky" | custom-call | tf_op jit(solution)/shard_map/jit(cholesky)/cholesky | solution.py:102
  385.3 9.9 %custom-call.31 = f32[1,128,128]{1,2,0:T(8,128)S(1)} custom-call(f32[1,128,128]{2,1,0:T(8,128)S(1)} %get-tuple-element.52), custom_call_target="InvertDiagBlocksLowerTriangular" | custom-call | tf_op jit(solution)/shard_map/jit(cholesky)/cholesky | solution.py:102
  396.0 11.7 %cholesky.238 = f32[128,128]{1,0:T(8,128)S(1)} custom-call(f32[128,128]{1,0:T(8,128)S(1)} %cholesky.275), custom_call_target="Cholesky" | custom-call | tf_op jit(solution)/shard_map/jit(cholesky)/cholesky | solution.py:102
  407.7 9.8 %custom-call.32 = f32[1,128,128]{1,2,0:T(8,128)S(1)} custom-call(f32[1,128,128]{2,1,0:T(8,128)S(1)} %get-tuple-element.49), custom_call_target="InvertDiagBlocksLowerTriangular" | custom-call | tf_op jit(solution)/shard_map/jit(cholesky)/cholesky | solution.py:102
  418.1 11.9 %cholesky.255 = f32[128,128]{1,0:T(8,128)S(1)} custom-call(f32[128,128]{1,0:T(8,128)S(1)} %convolution_subtract_fusion.9), custom_call_target="Cholesky" | custom-call | tf_op jit(solution)/shard_map/jit(cholesky)/cholesky | solution.py:102
  436.0 10.9 %while.4 = (s32[]{:T(128)}, f32[512,512]{1,0:T(8,128)S(1)}, s32[4,2]{0,1:T(2,128)S(1)}, f32[4,128,128]{2,1,0:T(8,128)}, s32[]{:T(128)}) while((s32[]{:T(128)}, f32[512,512]{1,0:T(8,128)S(1)}, s32[4,2]{0,1:T(2,128)S(1)}, f32[4,128,128]{2,1,0:T(8,128)}, s32[]{:T(128)}) %tuple.46), condition=%wide.while_cond, body=%wide.while_body.sunk | while | flops 2 | bytes 132205 | solution.py:103
  439.4 2.1 bitcast_dynamic-update-slice_fusion.2
  446.9 40.1 %custom-call.34 = f32[4,128,128]{1,2,0:T(8,128)S(1)} custom-call(f32[4,128,128]{2,1,0:T(8,128)} %get-tuple-element.17), custom_call_target="InvertDiagBlocksLowerTriangular" | custom-call | tf_op jit(solution)/shard_map/jit(_solve_triangular)/triangular_solve | solution.py:103
  (81 shorter events, 31.3 us)
Async XLA Ops:
  7.2 69.1 %all-gather.5.cloned.1.call-start = ((), (), s32[]{:S(2)}) async-start(), calls=%async_computation.2 | async-start | bytes 4718592 | tf_op jit(solution)/shard_map/all_gather | solution.py:21
  19.2 216.5 %all-gather.7.cloned.1.call-start = ((), (), s32[]{:S(2)}) async-start(), calls=%async_computation.3 | async-start | bytes 11141120 | tf_op jit(solution)/shard_map/all_gather | solution.py:76
  78.8 156.9 %copy-start.2 = (f32[1024]{0:T(1024)S(1)}, f32[1024]{0:T(1024)}, u32[]{:S(2)}) copy-start(f32[1024]{0:T(1024)} %param.6) | copy-start | bytes 12292
  251.9 39.1 %all-to-all-start = ((f32[16,160,160]{1,2,0:T(8,128)}), f32[16,160,160]{1,2,0:T(8,128)S(1)}, u32[]{:S(2)}, u32[]{:S(2)}) async-start(f32[16,160,160]{1,2,0:T(8,128)} %copy.34), calls=%async_computation | async-start | bytes 5242880 | tf_op jit(solution)/shard_map/all_to_all | solution.py:39
  257.6 90.6 %all-gather.9.cloned.1.call-start = ((), (), s32[]{:S(2)}) async-start(), calls=%async_computation.4 | async-start | bytes 1114112 | tf_op jit(solution)/shard_map/all_gather | solution.py:101
  291.3 49.0 %copy-start.1 = (f32[160,160]{1,0:T(8,128)}, f32[160,160]{1,0:T(8,128)S(1)}, u32[]{:S(2)}) copy-start(f32[160,160]{1,0:T(8,128)S(1)} %convert_add_fusion) | copy-start | bytes 307204
  337.7 0.8 copy-start
Sparse Core Ops, SparseCore 0:
  19.3 56.9 all-gather.4
  81.2 154.4 all-gather.6
  313.8 34.3 all-gather.8
